TPU v7x, 128 devices: a whole 4x4x4 slice. The times are simulated.
128 devices in a mesh: row: 16 (over x, z), col: 8 (over y, core).
Axes of the slice: x: 4, y: 4, z: 4, core: 2. Of those that a mesh axis runs over, the one named last changes fastest.
Arguments:
- tokens: bfloat16 [512, 256, 384], P('row', 'col'), may hold values from -6 to 6
- first_gain: float32 [384], replicated, may hold values from 0.1 to 1.9
- second_gain: float32 [384], replicated, may hold values from 0.1 to 1.9
- joint_weight: bfloat16 [384, 1152], replicated, may hold values from -0.3125 to 0.3125
- merge_weight: bfloat16 [384, 384], replicated, may hold values from -0.3125 to 0.3125
- expand_weight: bfloat16 [384, 1536], replicated, may hold values from -0.3125 to 0.3125
- shrink_weight: bfloat16 [1536, 384], replicated, may hold values from -0.15625 to 0.15625
- relative_bias: float32 [12, 64, 64], replicated, may hold values from -4 to 270
- lateral_weight: bfloat16 [384, 256], replicated, may hold values from -0.3125 to 0.3125
- conv_weight: bfloat16 [4, 2304, 256], replicated, may hold values from -0.125 to 0.125
- mask_weight: bfloat16 [256], replicated, may hold values from -0.375 to 0.375
- box_geometry: int32 [16, 8, 16, 4], P('row', 'col'), may hold values from 0 to 18, as said below
- box_counts: int32 [16, 8], P('row', 'col'), may hold values from 0 to 16, as said below
- box_owner: int32 [16, 8, 16], P('row', 'col'), may hold values from -1 to 15, as said below
- soft_target: bfloat16 [16, 8, 16, 196], P('row', 'col'), may hold values from 0 to 1
Outputs:
- features: bfloat16 [512, 256, 256], P('row', 'col')
- feature_grad: float32 [512, 256, 256], P('row', 'col')
- mask_logits: float32 [16, 8, 8, 196], P('row', 'col')
Inputs may be any that keep to these rules, and one draw needn't show every extreme that they name: `box_geometry`: components are top from 0 to 18, left from 0 to 18, height and width from 4 to 14; every slot, used or not, holds such a box. `box_counts`: the counts of one tile column sum to 8 times the tiles along the column; some tile of every column holds exactly 16 boxes. `box_owner`: A slot at or beyond its tile's count holds -1, a used slot an owner in its tile column; every owner is named by exactly 8 boxes of its column, and a tile names one owner at most 1 times, a bound reached by every tile holding 16 boxes.
All inputs are finite; a program needn't handle non-finite values.
Results may differ from a plain program's by a relative error of at most 0.02.
Values may be sent and summed in bfloat16 or wider, within the bound.
A program may use at most 128 MiB of HBM per device.

v0:
```python
import functools
import jax
import jax.numpy as jnp
from jax import lax
from jax.experimental import pallas as pl
from jax.experimental.pallas import tpu as pltpu
from jax.sharding import PartitionSpec as P

CROP = 14
BOX_OWN = 8
EPSILON = 1e-05
G1 = 0.7978845608028654
G2 = G1 * 0.044715
ROWS = 224
MESH = pl.DeviceIdType.MESH


def norm_rows(x, gain):
    x = x - jnp.mean(x, axis=-1, keepdims=True)
    return x * lax.rsqrt(jnp.mean(x * x, axis=-1, keepdims=True) + EPSILON) * gain


def neighbours():
    row_at, row_n = lax.axis_index("row"), lax.axis_size("row")
    col_at, col_n = lax.axis_index("col"), lax.axis_size("col")
    found = []
    for dr in (-1, 0, 1):
        for dc in (-1, 0, 1):
            if dr == 0 and dc == 0:
                continue
            there = None
            for d, at, n in ((dr, row_at, row_n), (dc, col_at, col_n)):
                if d:
                    ok = at > 0 if d < 0 else at < n - 1
                    there = ok if there is None else there & ok
            found.append((dr, dc, there, (row_at + dr, col_at + dc)))
    return found


def swin_kernel(
    tok, cols, g1, g2, wj_h, wm_h, we_h, ws_h, rb_h, wl_h, out,
    wj, wm, we, ws, rb, wl, E, J, ME, BB, ON,
    top, bottom, left, right, corner, send_sem, recv_sem, load_sem,
):
    f32, bf16 = jnp.float32, jnp.bfloat16
    row_at, row_n = lax.axis_index("row"), lax.axis_size("row")
    col_at, col_n = lax.axis_index("col"), lax.axis_size("col")
    loads = [
        pltpu.make_async_copy(src, dst, load_sem.at[n])
        for n, (src, dst) in enumerate(
            ((wj_h, wj), (rb_h, rb), (wm_h, wm), (we_h, we), (ws_h, ws), (wl_h, wl))
        )
    ]
    for load in loads:
        load.start()
    around = neighbours()
    barrier = pltpu.get_barrier_semaphore()
    for dr, dc, there, peer in around:

        @pl.when(there)
        def _(peer=peer):
            pl.semaphore_signal(barrier, inc=1, device_id=peer, device_id_type=MESH)

    near_rows = jnp.where(row_at > 0, 1, 0) + jnp.where(row_at < row_n - 1, 1, 0) + 1
    near_cols = jnp.where(col_at > 0, 1, 0) + jnp.where(col_at < col_n - 1, 1, 0) + 1
    pl.semaphore_wait(barrier, near_rows * near_cols - 1)

    def parts(dr, dc):
        if dc == 0:
            return (tok.at[0:4], bottom) if dr < 0 else (tok.at[28:32], top)
        side = cols.at[0] if dc < 0 else cols.at[1]
        if dr == 0:
            return (side, right) if dc < 0 else (side, left)
        piece = side.at[0:16] if dr < 0 else side.at[112:128]
        return piece, corner.at[(0 if dr > 0 else 2) + (0 if dc > 0 else 1)]

    def copy_to(n, dr, dc, peer):
        src, dst = parts(dr, dc)
        return pltpu.make_async_remote_copy(
            src_ref=src, dst_ref=dst, send_sem=send_sem.at[n], recv_sem=recv_sem.at[n],
            device_id=peer, device_id_type=MESH,
        )

    for n, (dr, dc, there, peer) in enumerate(around):

        @pl.when(there)
        def _(n=n, dr=dr, dc=dc, peer=peer):
            copy_to(n, dr, dc, peer).start()

    def fill(r, carry):
        E[r + 4, 4:36, :] = tok[r].astype(f32)
        return carry

    lax.fori_loop(0, 32, fill, 0)
    loads[0].wait()
    loads[1].wait()
    for c in range(6):
        BB[c] = jnp.concatenate([rb[2 * c], rb[2 * c + 1]], axis=1)
    lane = lax.broadcasted_iota(jnp.int32, (64, 128), 1)
    head_of = lane // 32
    zero = jnp.zeros((64, 128), bf16)
    for h in range(4):
        ON[h * 64 : (h + 1) * 64] = jnp.where(head_of == h, 1.0, 0.0).astype(bf16)
    low = lane < 64
    qi = lax.broadcasted_iota(jnp.int32, (64, 128), 0)
    kj = lane % 64
    row_cut = (qi // 32) != (kj // 32)
    col_cut = ((qi // 4) % 2) != ((kj // 4) % 2)

    def windows(wi, across):
        first, last = across[0], across[-1]
        count = len(across)
        if count == last - first + 1:
            x = E[pl.ds(wi * 8, 8), first * 8 : (last + 1) * 8, :]
        else:
            x = jnp.concatenate([E[pl.ds(wi * 8, 8), j * 8 : (j + 1) * 8, :] for j in across], axis=1)
        x = norm_rows(x, g1[...].reshape(1, 1, 384))
        m = jnp.concatenate(
            [x[:, n * 8 : (n + 1) * 8, :].reshape(64, 384) for n in range(count)], axis=0
        ).astype(bf16)
        top_row = count * 64
        J[0:top_row, 0:384] = (
            jnp.dot(m, wj[:, 0:384], preferred_element_type=f32) * 32**-0.5
        ).astype(bf16)
        J[0:top_row, 384:1152] = jnp.dot(m, wj[:, 384:1152], preferred_element_type=f32).astype(bf16)
        row_flag = ((wi == 0) & (row_at == 0)) | ((wi == 4) & (row_at == row_n - 1))
        for n, j in enumerate(across):
            cut = row_cut & row_flag
            if j == 0:
                cut = cut | (col_cut & (col_at == 0))
            if j == 4:
                cut = cut | (col_cut & (col_at == col_n - 1))
            sl = slice(n * 64, (n + 1) * 64)
            for g in range(3):
                q = J[sl, g * 128 : (g + 1) * 128]
                k = J[sl, 384 + g * 128 : 384 + (g + 1) * 128]
                v = J[sl, 768 + g * 128 : 768 + (g + 1) * 128]
                kb = jnp.concatenate([jnp.where(head_of == h, k, zero) for h in range(4)], axis=0)
                s = lax.dot_general(q, kb, (((1,), (1,)), ((), ())), preferred_element_type=f32)
                es = []
                for c in range(2):
                    b = s[:, c * 128 : (c + 1) * 128] + BB[2 * g + c]
                    b = jnp.where(cut, -1e9, b)
                    m0 = jnp.max(jnp.where(low, b, -3e38), axis=1, keepdims=True)
                    m1 = jnp.max(jnp.where(low, -3e38, b), axis=1, keepdims=True)
                    es.append(jnp.exp(b - jnp.where(low, m0, m1)).astype(bf16))
                p = jnp.concatenate(es, axis=1)
                vb = jnp.concatenate([jnp.where(head_of == h, v, zero) for h in range(4)], axis=0)
                o = jnp.dot(p, jnp.concatenate([vb, ON[...]], axis=1), preferred_element_type=f32)
                o = o[:, 0:128] / o[:, 128:256]
                ME[pl.ds(wi * 8, 8), j * 8 : (j + 1) * 8, g * 128 : (g + 1) * 128] = o.reshape(8, 8, 128)

    def inner(n, carry):
        windows(n + 1, (1, 2, 3))
        return carry

    lax.fori_loop(0, 3, inner, 0)

    def land(dr, dc):
        rows = 0 if dr < 0 else 36
        if dc == 0:
            src = top if dr < 0 else bottom
            for r in range(4):
                yield (rows + r, slice(4, 36), lambda r=r: src[r].astype(f32))
            return
        span = slice(0, 4) if dc < 0 else slice(36, 40)
        if dr == 0:
            src = left if dc < 0 else right
            for h in range(8):
                for r in range(4):
                    yield (
                        4 + h * 4 + r, span,
                        lambda h=h, r=r: src[h * 16 : (h + 1) * 16].astype(f32)[r * 4 : (r + 1) * 4],
                    )
            return
        piece = corner.at[(0 if dr < 0 else 2) + (0 if dc < 0 else 1)]
        for r in range(4):
            yield (rows + r, span, lambda r=r: piece[...].astype(f32)[r * 4 : (r + 1) * 4])

    for n, (dr, dc, there, peer) in enumerate(around):

        @pl.when(there)
        def _(n=n, dr=dr, dc=dc, peer=peer):
            copy_to(n, dr, dc, peer).wait_send()
            copy_to(len(around) - 1 - n, -dr, -dc, peer).wait_recv()
            for r, span, value in land(dr, dc):
                E[r, span, :] = value()

        @pl.when(jnp.logical_not(there))
        def _(dr=dr, dc=dc):
            for r, span, value in land(dr, dc):
                E[r, span, :] = jnp.zeros((span.stop - span.start, 384), f32)

    def sides(n, carry):
        windows(n + 1, (0, 4))
        return carry

    lax.fori_loop(0, 3, sides, 0)

    def ends(n, carry):
        windows(n * 4, (0, 1, 2, 3, 4))
        return carry

    lax.fori_loop(0, 2, ends, 0)
    for load in loads[2:]:
        load.wait()
    R = 16

    def tail(c, carry):
        r0 = c * R
        mixed = jnp.concatenate([ME[r0 + q + 4, 4:36, :] for q in range(R)], axis=0).astype(bf16)
        t = jnp.concatenate([tok[r0 + q] for q in range(R)], axis=0).astype(f32)
        res = t + jnp.dot(mixed, wm[...], preferred_element_type=f32)
        n2 = norm_rows(res, g2[...].reshape(1, 384)).astype(bf16)
        h = jnp.dot(n2, we[...], preferred_element_type=f32)
        h = (h * (0.5 + 0.5 * jnp.tanh(h * (G1 + G2 * (h * h))))).astype(bf16)
        b = (res + jnp.dot(h, ws[...], preferred_element_type=f32)).astype(bf16)
        f = jnp.dot(b, wl[...], preferred_element_type=f32).astype(bf16)
        for q in range(R):
            out[r0 + q] = f[q * 32 : (q + 1) * 32]
        return carry

    lax.fori_loop(0, 32 // R, tail, 0)


def swin(tok, cols, g1, g2, wj, wm, we, ws, rb, wl):
    V = pl.BlockSpec(memory_space=pltpu.VMEM)
    A = pl.BlockSpec(memory_space=pl.ANY)
    weights = (wj, wm, we, ws, rb, wl)
    return pl.pallas_call(
        swin_kernel,
        out_shape=jax.ShapeDtypeStruct((32, 32, 256), jnp.bfloat16),
        in_specs=[V] * 4 + [A] * 6,
        out_specs=V,
        scratch_shapes=[pltpu.VMEM(w.shape, w.dtype) for w in weights]
        + [
            pltpu.VMEM((40, 40, 384), jnp.float32),
            pltpu.VMEM((320, 1152), jnp.bfloat16),
            pltpu.VMEM((40, 40, 384), jnp.float32),
            pltpu.VMEM((6, 64, 128), jnp.float32),
            pltpu.VMEM((256, 128), jnp.bfloat16),
            pltpu.VMEM((4, 32, 384), jnp.bfloat16),
            pltpu.VMEM((4, 32, 384), jnp.bfloat16),
            pltpu.VMEM((128, 384), jnp.bfloat16),
            pltpu.VMEM((128, 384), jnp.bfloat16),
            pltpu.VMEM((4, 16, 384), jnp.bfloat16),
            pltpu.SemaphoreType.DMA((8,)),
            pltpu.SemaphoreType.DMA((8,)),
            pltpu.SemaphoreType.DMA((6,)),
        ],
        compiler_params=pltpu.CompilerParams(
            vmem_limit_bytes=63 << 20, collective_id=0, has_side_effects=True
        ),
    )(tok, cols, g1, g2, wj, wm, we, ws, rb, wl)


def gelu_pair(x):
    x2 = x * x
    inner = x * (G1 + (G2) * x2)
    th = jnp.tanh(inner)
    half = 0.5 + 0.5 * th
    act = x * half
    slope = half + (0.5 * x) * (1.0 - th * th) * (G1 + (3.0 * G2) * x2)
    return act, slope

def mask_kernel(U, gs, cs, geom, own, soft, feat, w_h, mw, fg, rt, feat_out, X, Y, D, tgt, lg, w, sem):
    f32, bf16 = jnp.float32, jnp.bfloat16
    cnt = cs[0, 0]
    loads = [pltpu.make_async_copy(w_h.at[n], w.at[n], sem.at[n]) for n in range(4)]
    for load in loads:
        load.start()
    store = pltpu.make_async_copy(feat, feat_out, sem.at[4])
    store.start()
    zrow = jnp.zeros((256, 256), bf16)
    for B in (X, Y):
        B[0] = zrow
        B[15] = zrow
        for u in range(1, 15):
            B[u, 0:16, :] = zrow[0:16]
            B[u, 240:256, :] = zrow[0:16]
    g = geom[0, 0]
    valid = lax.broadcasted_iota(jnp.int32, (16, 1), 0) < cnt
    rep = lambda col: jnp.concatenate([col] * 14, axis=0)
    lefts, widths = rep(g[:, 1:2]), rep(g[:, 3:4])
    heights = rep(jnp.where(valid, g[:, 2:3], 0))
    row = lax.broadcasted_iota(jnp.int32, (ROWS, 1), 0)
    vv, kk = row // 16, row % 16
    target = jnp.where(vv < widths, kk * 32 + lefts + vv, -1)
    lane = lax.broadcasted_iota(jnp.int32, (ROWS, 512), 1)
    pick = jnp.where(lane == target, 1.0, 0.0).astype(bf16)
    in_w = vv < widths

    soft_rows = soft[0, 0]
    cell = lax.broadcasted_iota(jnp.int32, (CROP * CROP, 128), 0)
    step = lax.broadcasted_iota(jnp.int32, (CROP * CROP, 128), 1)
    for v in range(CROP):
        spread = jnp.where(cell == step * CROP + v, 1.0, 0.0).astype(bf16)
        tgt[v * 16:(v + 1) * 16] = jnp.dot(soft_rows, spread, preferred_element_type=f32)

    def gather(u, c):
        strips = jnp.concatenate([feat[gs[0, 0, k, 0] + u] for k in range(16)], axis=0)
        crop = jnp.dot(pick, strips, preferred_element_type=f32)
        crop = jnp.where(u < heights, crop, 0.0)
        X[u + 1, 16:240, :] = crop.astype(bf16)
        return c
    lax.fori_loop(0, 14, gather, 0)

    def fwd(src, dst, l):
        loads[l].wait()
        def body(i, c):
            u0 = i * U
            cols = []
            for s in range(3):
                for t in range(3):
                    cols.append(jnp.concatenate([src[u0 + q + s, t * 16:t * 16 + ROWS, :] for q in range(U)], axis=0))
            pre = jnp.dot(jnp.concatenate(cols, axis=1), w[l], preferred_element_type=f32)
            act, slope = gelu_pair(pre)
            for q in range(U):
                a = act[q * ROWS:(q + 1) * ROWS].astype(bf16)
                sl = slope[q * ROWS:(q + 1) * ROWS]
                if l < 3:
                    dst[u0 + q + 1, 16:240, :] = a
                    D[l, u0 + q] = sl.astype(bf16)
                else:
                    u = u0 + q
                    m = mw[...].astype(f32).reshape(1, 256)
                    logit = jnp.sum(a.astype(f32) * m, axis=1, keepdims=True)
                    sel = lax.broadcasted_iota(jnp.int32, (ROWS, 128), 1) == u
                    lg[...] = jnp.where(sel, logit, lg[...])
                    tg = jnp.sum(jnp.where(sel, tgt[...], 0.0), axis=1, keepdims=True)
                    gl = jnp.where(in_w & (u < heights), 128.0 * (jax.nn.sigmoid(logit) - tg), 0.0)
                    dst[u + 1, 16:240, :] = (gl * m * sl).astype(bf16)
            return c
        lax.fori_loop(0, 14 // U, body, 0)

    lg[...] = jnp.zeros_like(lg)
    fwd(X, Y, 0)
    fwd(Y, X, 1)
    fwd(X, Y, 2)
    fwd(Y, X, 3)

    spot = lax.broadcasted_iota(jnp.int32, (128, 256), 1)
    from_u = lax.broadcasted_iota(jnp.int32, (128, 256), 0)

    def halves(a):
        hi = a.astype(bf16)
        return hi, (a - hi.astype(f32)).astype(bf16)

    flat = jnp.zeros((16, 256), f32)
    for v in range(CROP):
        spread = jnp.where((spot == from_u * CROP + v) & (from_u < CROP), 1.0, 0.0).astype(bf16)
        for part in halves(lg[v * 16:(v + 1) * 16]):
            flat = flat + jnp.dot(part, spread, preferred_element_type=f32)
    flat = jnp.where(lax.broadcasted_iota(jnp.int32, (16, 256), 1) < CROP * CROP, flat, 1.0)
    used = lax.broadcasted_iota(jnp.int32, (16, 16), 1) < cnt
    sent = jnp.where((own[0] == lax.broadcasted_iota(jnp.int32, (16, 16), 0)) & used, 1.0, 0.0).astype(bf16)
    routed = jnp.zeros((16, 256), f32)
    for part in halves(flat):
        routed = routed + jnp.dot(sent, part, preferred_element_type=f32)
    for o in range(16):
        rt[o] = routed[o:o + 1]

    fg[...] = jnp.zeros_like(fg)

    def bwd(src, dst, l):
        def body(i, c):
            u0 = i * U
            acc = None
            for s in range(3):
                for t in range(3):
                    a = jnp.concatenate([src[u0 + q + 2 - s, (2 - t) * 16:(2 - t) * 16 + ROWS, :] for q in range(U)], axis=0)
                    tap = 3 * s + t
                    d = lax.dot_general(a, w[l, tap * 256:(tap + 1) * 256, :], (((1,), (1,)), ((), ())), preferred_element_type=f32)
                    acc = d if acc is None else acc + d
            for q in range(U):
                gq = acc[q * ROWS:(q + 1) * ROWS]
                if l > 0:
                    dst[u0 + q + 1, 16:240, :] = (gq * D[l - 1, u0 + q].astype(f32)).astype(bf16)
                else:
                    u = u0 + q
                    gq = jnp.where(u < heights, gq, 0.0).astype(bf16)
                    z = lax.dot_general(pick, gq, (((0,), (0,)), ((), ())), preferred_element_type=f32)
                    for k in range(16):
                        fg[gs[0, 0, k, 0] + u] += z[k * 32:(k + 1) * 32]
            return c
        lax.fori_loop(0, 14 // U, body, 0)
    bwd(X, Y, 3)
    bwd(Y, X, 2)
    bwd(X, Y, 1)
    bwd(Y, X, 0)
    store.wait()

def mask_head(geometry, count, owner, soft, feat, conv_w, mask_w):
    V = pl.BlockSpec(memory_space=pltpu.VMEM)
    S = pl.BlockSpec(memory_space=pltpu.SMEM)
    A = pl.BlockSpec(memory_space=pl.ANY)
    return pl.pallas_call(
        functools.partial(mask_kernel, 7),
        out_shape=(
            jax.ShapeDtypeStruct((32, 32, 256), jnp.float32),
            jax.ShapeDtypeStruct((16, 1, 256), jnp.float32),
            jax.ShapeDtypeStruct((32, 32, 256), jnp.bfloat16),
        ),
        in_specs=[S, S, V, V, V, V, A, V],
        out_specs=(V, V, A),
        scratch_shapes=[
            pltpu.VMEM((16, 256, 256), jnp.bfloat16),
            pltpu.VMEM((16, 256, 256), jnp.bfloat16),
            pltpu.VMEM((3, 14, ROWS, 256), jnp.bfloat16),
            pltpu.VMEM((ROWS, 128), jnp.float32),
            pltpu.VMEM((ROWS, 128), jnp.float32),
            pltpu.VMEM((4, 2304, 256), jnp.bfloat16),
            pltpu.SemaphoreType.DMA((5,)),
        ],
        compiler_params=pltpu.CompilerParams(vmem_limit_bytes=63 << 20),
    )(geometry, count, geometry, owner, soft, feat, conv_w, mask_w)


def deal_kernel(outgoing, out, recv, send_sem, recv_sem):
    me, n = lax.axis_index("row"), lax.axis_size("row")
    col = lax.axis_index("col")
    barrier = pltpu.get_barrier_semaphore()
    for d in range(1, 16):
        pl.semaphore_signal(
            barrier, inc=1, device_id=(lax.rem(me + d, n), col), device_id_type=MESH
        )
    pl.semaphore_wait(barrier, 15)

    def copy_to(d, slot):
        peer = lax.rem(me + d, n)
        return pltpu.make_async_remote_copy(
            src_ref=outgoing.at[peer], dst_ref=recv.at[slot],
            send_sem=send_sem.at[d], recv_sem=recv_sem.at[d],
            device_id=(peer, col), device_id_type=MESH,
        )

    for d in range(1, 16):
        copy_to(d, me).start()
    recv[me] = outgoing[me]
    for d in range(1, 16):
        copy_to(d, lax.rem(me + n - d, n)).wait()
    got = jnp.concatenate([recv[i] for i in range(16)], axis=0)
    flag = jnp.where(got[:, 255:256] > 0.5, 1.0, 0.0)
    later = lax.broadcasted_iota(jnp.int32, (16, 16), 0) > lax.broadcasted_iota(
        jnp.int32, (16, 16), 1
    )
    place = jnp.dot(
        jnp.where(later, 1.0, 0.0).astype(jnp.bfloat16),
        jnp.broadcast_to(flag, (16, 128)).astype(jnp.bfloat16),
        preferred_element_type=jnp.float32,
    )[:, 0:1]
    rows = [
        jnp.sum(jnp.where((place == float(i)) & (flag > 0.5), got, 0.0), axis=0, keepdims=True)
        for i in range(BOX_OWN)
    ]
    out[0, 0] = jnp.concatenate(rows, axis=0)[:, 0 : CROP * CROP]


def deal_logits(outgoing):
    V = pl.BlockSpec(memory_space=pltpu.VMEM)
    return pl.pallas_call(
        deal_kernel,
        out_shape=jax.ShapeDtypeStruct((1, 1, BOX_OWN, CROP * CROP), jnp.float32),
        in_specs=[V],
        out_specs=V,
        scratch_shapes=[
            pltpu.VMEM((16, 1, 256), jnp.float32),
            pltpu.SemaphoreType.DMA((16,)),
            pltpu.SemaphoreType.DMA((16,)),
        ],
        compiler_params=pltpu.CompilerParams(collective_id=1, has_side_effects=True),
    )(outgoing)


def shards(
    tokens,
    first_gain,
    second_gain,
    joint_weight,
    merge_weight,
    expand_weight,
    shrink_weight,
    relative_bias,
    lateral_weight,
    conv_weight,
    mask_weight,
    box_geometry,
    box_counts,
    box_owner,
    soft_target,
):
    cols = jnp.stack([tokens[:, :4].reshape(128, -1), tokens[:, 28:].reshape(128, -1)])
    features = swin(
        tokens, cols, first_gain, second_gain, joint_weight, merge_weight,
        expand_weight, shrink_weight, relative_bias, lateral_weight,
    )
    feature_grad, outgoing, features = mask_head(
        box_geometry, box_counts, box_owner, soft_target, features, conv_weight, mask_weight
    )
    return (features, feature_grad, deal_logits(outgoing))


def solution(mesh):
    placed = (
        P("row", "col", None),
        P(),
        P(),
        P(),
        P(),
        P(),
        P(),
        P(),
        P(),
        P(),
        P(),
        P("row", "col", None, None),
        P("row", "col"),
        P("row", "col", None),
        P("row", "col", None, None),
    )
    return jax.shard_map(
        shards,
        mesh=mesh,
        in_specs=placed,
        out_specs=(P("row", "col", None), P("row", "col", None), P("row", "col", None, None)),
        check_vma=False,
    )
```

profile of v0, /device:TPU:24, one launch (start us, length us, event | category | flops | bytes accessed | tf_op | source)
XLA Modules:
  0.0 91.1 jit_solution(2255814375424974292)
XLA Ops:
  1.3 1.4 %copy.20.gs.geom = s32[1,1,16,4]{3,2,1,0:T(8,128)} copy(s32[1,1,16,4]{2,3,1,0:T(4,128)} %param.26) | data formatting | bytes 512 | tf_op args[11]
  2.6 1.1 %fusion = (bf16[32,4,384]{2,1,0:T(4,128)(2,1)S(1)}, bf16[32,4,384]{2,1,0:T(4,128)(2,1)S(1)}) fusion(bf16[32,32,384]{2,1,0:T(8,128)(2,1)} %tok.1), kind=kLoop, calls=%fused_computation.1 | loop fusion | bytes 393216 | tf_op jit(solution)/shard_map/slice | solution.py:492
  3.8 0.7 pad_maximum_fusion.cols
  4.5 21.5 %shard_map.166.feat = bf16[32,32,256]{2,1,0:T(8,128)(2,1)} custom-call(bf16[32,32,384]{2,1,0:T(8,128)(2,1)} %tok.1, bf16[2,128,384]{2,1,0:T(8,128)(2,1)} %pad_maximum_fusion.cols, f32[384]{0:T(512)} %g1.1, f32[384]{0:T(512)} %g2.1, bf16[384,1152]{1,0:T(8,128)(2,1)} %wj_h.1, bf16[384,384]{1,0:T(8,128)(2,1)} %wm_h.1, bf16[384,1536]{1,0:T(8,128)(2,1)} %we_h.1, ...), custom_call_target="tpu_custom_call" | custom-call | tf_op jit(solution)/shard_map/pallas_call | solution.py:230
  26.1 50.2 %shard_map.167 = (f32[32,32,256]{2,1,0:T(8,128)}, f32[16,1,256]{2,1,0:T(1,128)}, bf16[32,32,256]{2,1,0:T(8,128)(2,1)}) custom-call(s32[1,1,16,4]{3,2,1,0:T(8,128)} %copy.20.gs.geom, s32[1,1]{1,0:T(1,128)S(6)} %copy.23.cs, s32[1,1,16,4]{3,2,1,0:T(8,128)} %copy.20.gs.geom, s32[1,1,16]{2,1,0:T(1,128)} %own.1, bf16[1,1,16,196]{3,2,1,0:T(8,128)(2,1)} %soft.1, ...), custom_call_target="tpu_custom_call" | custom-call | tf_op jit(solution)/shard_map/pallas_call | solution.py:397
  76.3 13.5 %shard_map.168 = f32[1,1,8,196]{3,2,1,0:T(8,128)} custom-call(f32[16,1,256]{2,1,0:T(1,128)} %get-tuple-element.8.outgoing), custom_call_target="tpu_custom_call" | custom-call | tf_op jit(solution)/shard_map/pallas_call | solution.py:461
  89.8 1.3 %copy.24 = f32[1,1,8,196]{3,2,1,0:T(8,128)} copy(f32[1,1,8,196]{3,2,1,0:T(8,128)} %shard_map.168) | data formatting | bytes 12544
  (2 shorter events, 0.1 us)
where the time goes:
time: 91.4 us; the launch traced here: 91.1 us
  Pallas kernels  85.2 us (93%)
  local copies, waits for them, and re-layouts  3.81 us (4%)
  between operations  1.31 us (1%)
    pallas_call x1, Pallas kernels, mask_head(): pl.pallas_call(functools.partial(mask_kernel, 7), out_shape=(jax.ShapeDty...  50.2 us
    pallas_call x1, Pallas kernels, swin(): pl.pallas_call(swin_kernel, out_shape=jax.ShapeDtypeStruct((32, 32, 256),...  21.5 us
    pallas_call x1, Pallas kernels, deal_logits(): pl.pallas_call(deal_kernel, out_shape=jax.ShapeDtypeStruct((1, 1, BOX_OWN...  13.5 us
    unnamed x2, local copies, waits for them, and re-layouts  2.65 us

commit v1 on v0

--- a/solution.py
+++ b/solution.py
@@ -38,7 +38,7 @@
 
 
 def swin_kernel(
-    tok, cols, g1, g2, wj_h, wm_h, we_h, ws_h, rb_h, wl_h, out,
+    tok, g1, g2, wj_h, wm_h, we_h, ws_h, rb_h, wl_h, out,
     wj, wm, we, ws, rb, wl, E, J, ME, BB, ON,
     top, bottom, left, right, corner, send_sem, recv_sem, load_sem,
 ):
@@ -68,10 +68,10 @@
     def parts(dr, dc):
         if dc == 0:
             return (tok.at[0:4], bottom) if dr < 0 else (tok.at[28:32], top)
-        side = cols.at[0] if dc < 0 else cols.at[1]
+        span = slice(0, 8) if dc < 0 else slice(24, 32)
         if dr == 0:
-            return (side, right) if dc < 0 else (side, left)
-        piece = side.at[0:16] if dr < 0 else side.at[112:128]
+            return tok.at[:, span], (right if dc < 0 else left)
+        piece = tok.at[0:4, span] if dr < 0 else tok.at[28:32, span]
         return piece, corner.at[(0 if dr > 0 else 2) + (0 if dc > 0 else 1)]
 
     def copy_to(n, dr, dc, peer):
@@ -163,19 +163,15 @@
             for r in range(4):
                 yield (rows + r, slice(4, 36), lambda r=r: src[r].astype(f32))
             return
-        span = slice(0, 4) if dc < 0 else slice(36, 40)
+        span, part = (slice(0, 4), slice(4, 8)) if dc < 0 else (slice(36, 40), slice(0, 4))
         if dr == 0:
             src = left if dc < 0 else right
-            for h in range(8):
-                for r in range(4):
-                    yield (
-                        4 + h * 4 + r, span,
-                        lambda h=h, r=r: src[h * 16 : (h + 1) * 16].astype(f32)[r * 4 : (r + 1) * 4],
-                    )
+            for r in range(32):
+                yield (4 + r, span, lambda r=r: src[r].astype(f32)[part])
             return
         piece = corner.at[(0 if dr < 0 else 2) + (0 if dc < 0 else 1)]
         for r in range(4):
-            yield (rows + r, span, lambda r=r: piece[...].astype(f32)[r * 4 : (r + 1) * 4])
+            yield (rows + r, span, lambda r=r: piece[r].astype(f32)[part])
 
     for n, (dr, dc, there, peer) in enumerate(around):
 
@@ -223,14 +219,14 @@
     lax.fori_loop(0, 32 // R, tail, 0)
 
 
-def swin(tok, cols, g1, g2, wj, wm, we, ws, rb, wl):
+def swin(tok, g1, g2, wj, wm, we, ws, rb, wl):
     V = pl.BlockSpec(memory_space=pltpu.VMEM)
     A = pl.BlockSpec(memory_space=pl.ANY)
     weights = (wj, wm, we, ws, rb, wl)
     return pl.pallas_call(
         swin_kernel,
         out_shape=jax.ShapeDtypeStruct((32, 32, 256), jnp.bfloat16),
-        in_specs=[V] * 4 + [A] * 6,
+        in_specs=[V] * 3 + [A] * 6,
         out_specs=V,
         scratch_shapes=[pltpu.VMEM(w.shape, w.dtype) for w in weights]
         + [
@@ -241,9 +237,9 @@
             pltpu.VMEM((256, 128), jnp.bfloat16),
             pltpu.VMEM((4, 32, 384), jnp.bfloat16),
             pltpu.VMEM((4, 32, 384), jnp.bfloat16),
-            pltpu.VMEM((128, 384), jnp.bfloat16),
-            pltpu.VMEM((128, 384), jnp.bfloat16),
-            pltpu.VMEM((4, 16, 384), jnp.bfloat16),
+            pltpu.VMEM((32, 8, 384), jnp.bfloat16),
+            pltpu.VMEM((32, 8, 384), jnp.bfloat16),
+            pltpu.VMEM((4, 4, 8, 384), jnp.bfloat16),
             pltpu.SemaphoreType.DMA((8,)),
             pltpu.SemaphoreType.DMA((8,)),
             pltpu.SemaphoreType.DMA((6,)),
@@ -251,19 +247,23 @@
         compiler_params=pltpu.CompilerParams(
             vmem_limit_bytes=63 << 20, collective_id=0, has_side_effects=True
         ),
-    )(tok, cols, g1, g2, wj, wm, we, ws, rb, wl)
+    )(tok, g1, g2, wj, wm, we, ws, rb, wl)
 
 
 def gelu_pair(x):
     x2 = x * x
-    inner = x * (G1 + (G2) * x2)
-    th = jnp.tanh(inner)
-    half = 0.5 + 0.5 * th
+    half = 0.5 + 0.5 * jnp.tanh(x * (G1 + G2 * x2))
     act = x * half
-    slope = half + (0.5 * x) * (1.0 - th * th) * (G1 + (3.0 * G2) * x2)
+    slope = half + act * (1.0 - half) * (2.0 * G1 + (6.0 * G2) * x2)
     return act, slope
 
-def mask_kernel(U, gs, cs, geom, own, soft, feat, w_h, mw, fg, rt, feat_out, X, Y, D, tgt, lg, w, sem):
+
+def halves(a):
+    hi = a.astype(jnp.bfloat16)
+    return hi, (a - hi.astype(jnp.float32)).astype(jnp.bfloat16)
+
+
+def mask_kernel(gs, cs, geom, own, soft, feat, w_h, mw, fg, rt, feat_out, A, T, D, tgt, lg, w, V, P, sem):
     f32, bf16 = jnp.float32, jnp.bfloat16
     cnt = cs[0, 0]
     loads = [pltpu.make_async_copy(w_h.at[n], w.at[n], sem.at[n]) for n in range(4)]
@@ -272,144 +272,197 @@
     store = pltpu.make_async_copy(feat, feat_out, sem.at[4])
     store.start()
     zrow = jnp.zeros((256, 256), bf16)
-    for B in (X, Y):
-        B[0] = zrow
-        B[15] = zrow
-        for u in range(1, 15):
-            B[u, 0:16, :] = zrow[0:16]
-            B[u, 240:256, :] = zrow[0:16]
+    A[0] = zrow
+    A[15] = zrow
+    for u in range(1, 15):
+        A[u, 0:16, :] = zrow[0:16]
+        A[u, 240:256, :] = zrow[0:16]
     g = geom[0, 0]
     valid = lax.broadcasted_iota(jnp.int32, (16, 1), 0) < cnt
-    rep = lambda col: jnp.concatenate([col] * 14, axis=0)
-    lefts, widths = rep(g[:, 1:2]), rep(g[:, 3:4])
-    heights = rep(jnp.where(valid, g[:, 2:3], 0))
+
+    def column(n):
+        same = lax.broadcasted_iota(jnp.int32, (16, 16), 0) == lax.broadcasted_iota(
+            jnp.int32, (16, 16), 1
+        )
+        return jnp.sum(jnp.where(same, g[n : n + 1], 0), axis=1, keepdims=True)
+
+    def rep(col):
+        return jnp.concatenate([col] * CROP, axis=0)
+
+    lefts, widths = rep(column(1)), rep(column(3))
+    heights = rep(jnp.where(valid, column(2), 0))
     row = lax.broadcasted_iota(jnp.int32, (ROWS, 1), 0)
     vv, kk = row // 16, row % 16
-    target = jnp.where(vv < widths, kk * 32 + lefts + vv, -1)
+    in_w = vv < widths
+    target = jnp.where(in_w, kk * 32 + lefts + vv, -1)
     lane = lax.broadcasted_iota(jnp.int32, (ROWS, 512), 1)
     pick = jnp.where(lane == target, 1.0, 0.0).astype(bf16)
-    in_w = vv < widths
 
     soft_rows = soft[0, 0]
     cell = lax.broadcasted_iota(jnp.int32, (CROP * CROP, 128), 0)
     step = lax.broadcasted_iota(jnp.int32, (CROP * CROP, 128), 1)
     for v in range(CROP):
         spread = jnp.where(cell == step * CROP + v, 1.0, 0.0).astype(bf16)
-        tgt[v * 16:(v + 1) * 16] = jnp.dot(soft_rows, spread, preferred_element_type=f32)
+        tgt[v * 16 : (v + 1) * 16] = jnp.dot(soft_rows, spread, preferred_element_type=f32)
 
     def gather(u, c):
-        strips = jnp.concatenate([feat[gs[0, 0, k, 0] + u] for k in range(16)], axis=0)
+        strips = jnp.concatenate([feat[gs[0, 0, 0, k] + u] for k in range(16)], axis=0)
         crop = jnp.dot(pick, strips, preferred_element_type=f32)
         crop = jnp.where(u < heights, crop, 0.0)
-        X[u + 1, 16:240, :] = crop.astype(bf16)
+        A[u + 1, 16:240, :] = crop.astype(bf16)
         return c
-    lax.fori_loop(0, 14, gather, 0)
-
-    def fwd(src, dst, l):
-        loads[l].wait()
-        def body(i, c):
-            u0 = i * U
-            cols = []
-            for s in range(3):
-                for t in range(3):
-                    cols.append(jnp.concatenate([src[u0 + q + s, t * 16:t * 16 + ROWS, :] for q in range(U)], axis=0))
-            pre = jnp.dot(jnp.concatenate(cols, axis=1), w[l], preferred_element_type=f32)
-            act, slope = gelu_pair(pre)
-            for q in range(U):
-                a = act[q * ROWS:(q + 1) * ROWS].astype(bf16)
-                sl = slope[q * ROWS:(q + 1) * ROWS]
-                if l < 3:
-                    dst[u0 + q + 1, 16:240, :] = a
-                    D[l, u0 + q] = sl.astype(bf16)
-                else:
-                    u = u0 + q
-                    m = mw[...].astype(f32).reshape(1, 256)
-                    logit = jnp.sum(a.astype(f32) * m, axis=1, keepdims=True)
-                    sel = lax.broadcasted_iota(jnp.int32, (ROWS, 128), 1) == u
-                    lg[...] = jnp.where(sel, logit, lg[...])
-                    tg = jnp.sum(jnp.where(sel, tgt[...], 0.0), axis=1, keepdims=True)
-                    gl = jnp.where(in_w & (u < heights), 128.0 * (jax.nn.sigmoid(logit) - tg), 0.0)
-                    dst[u + 1, 16:240, :] = (gl * m * sl).astype(bf16)
-            return c
-        lax.fori_loop(0, 14 // U, body, 0)
-
+
+    lax.fori_loop(0, CROP, gather, 0)
     lg[...] = jnp.zeros_like(lg)
-    fwd(X, Y, 0)
-    fwd(Y, X, 1)
-    fwd(X, Y, 2)
-    fwd(Y, X, 3)
+
+    def form(j):
+        for m in range(7):
+            d = [A[2 * m + i] for i in range(4)]
+            T[j, m] = (d[0] - d[2], d[1] + d[2], d[2] - d[1], d[1] - d[3])[j]
+
+    def taps(l):
+        for n in range(0, 768, 256):
+            a = w[l, n : n + 256].astype(f32) + w[l, 1536 + n : 1792 + n].astype(f32)
+            b = w[l, 768 + n : 1024 + n].astype(f32)
+            V[l, 0, n : n + 256] = (0.5 * (a + b)).astype(bf16)
+            V[l, 1, n : n + 256] = (0.5 * (a - b)).astype(bf16)
+
+    def kernel_of(l, j):
+        return (w.at[l, 0:768], V.at[l, 0], V.at[l, 1], w.at[l, 1536:2304])[j]
+
+    def shifted(j, t):
+        return jnp.concatenate([T[j, m, t * 16 : t * 16 + ROWS, :] for m in range(7)], axis=0)
+
+    def fwd_product(l, j):
+        lhs = jnp.concatenate([shifted(j, t) for t in range(3)], axis=1)
+        return jnp.dot(lhs, kernel_of(l, j)[...], preferred_element_type=f32)
+
+    def bwd_product(l, j):
+        ref = kernel_of(l, 3 - j if j in (0, 3) else j)
+        acc = None
+        for t in range(3):
+            d = lax.dot_general(
+                shifted(j, 2 - t), ref[t * 256 : (t + 1) * 256], (((1,), (1,)), ((), ())),
+                preferred_element_type=f32,
+            )
+            acc = d if acc is None else acc + d
+        return acc
+
+    def finish_fwd(l, u, pre):
+        act, slope = gelu_pair(pre)
+        A[u + 1, 16:240, :] = act.astype(bf16)
+        D[l, u] = slope.astype(bf16)
+
+    def finish_last(l, u, pre):
+        act, slope = gelu_pair(pre)
+        m = mw[...].astype(f32).reshape(1, 256)
+        logit = jnp.sum(act.astype(bf16).astype(f32) * m, axis=1, keepdims=True)
+        sel = lax.broadcasted_iota(jnp.int32, (ROWS, 128), 1) == u
+        lg[...] = jnp.where(sel, logit, lg[...])
+        tg = tgt[:, u : u + 1]
+        gl = jnp.where(in_w & (u < heights), 128.0 * (jax.nn.sigmoid(logit) - tg), 0.0)
+        A[u + 1, 16:240, :] = (gl * m * slope).astype(bf16)
+
+    def layer(l, product, finish, first, waiting, parity):
+        lead = 3 if first == 0 else 0
+        rest = 3 - lead
+        p1, p2, p_lead, p_rest = P.at[0], P.at[1], P.at[2 + parity], P.at[4 + parity]
+        form(lead)
+        p_lead[...] = product(l, lead)
+        waiting()
+        for j in (1, 2, rest):
+            form(j)
+        p1[...] = product(l, 1)
+        p2[...] = product(l, 2)
+        p_rest[...] = product(l, rest)
+
+        def done(odd, edge):
+            for m in range(7):
+                sl = slice(m * ROWS, (m + 1) * ROWS)
+                x = p1[sl] - p2[sl] - edge[sl] if odd else p1[sl] + p2[sl] + edge[sl]
+                finish(l, 2 * m + odd, x)
+
+        other = 1 - first
+        done(other, p_lead)
+        return other, lambda: done(first, p_rest), 1 - parity
+
+    loads[0].wait()
+    taps(0)
+    state = (0, lambda: None, 0)
+    for l in range(4):
+        state = layer(l, fwd_product, finish_last if l == 3 else finish_fwd, *state)
+        if l < 3:
+            loads[l + 1].wait()
+            taps(l + 1)
+    fg[...] = jnp.zeros_like(fg)
+    state[1]()
+
+    def products(l):
+        for j in range(4):
+            form(j)
+        for j in range(4):
+            P[j] = bwd_product(l, j)
+
+    def rows_of(m, odd):
+        sl = slice(m * ROWS, (m + 1) * ROWS)
+        return P[1, sl] - P[2, sl] - P[3, sl] if odd else P[0, sl] + P[1, sl] + P[2, sl]
+
+    def back(i, c):
+        l = 3 - i
+        products(l)
+        for u in range(CROP):
+            A[u + 1, 16:240, :] = (rows_of(u // 2, u % 2) * D[l - 1, u].astype(f32)).astype(bf16)
+        return c
+
+    lax.fori_loop(0, 3, back, 0)
+    products(0)
+    for u in range(CROP):
+        grad = jnp.where(u < heights, rows_of(u // 2, u % 2), 0.0).astype(bf16)
+        z = lax.dot_general(pick, grad, (((0,), (0,)), ((), ())), preferred_element_type=f32)
+        for k in range(16):
+            fg[gs[0, 0, 0, k] + u] += z[k * 32 : (k + 1) * 32]
 
     spot = lax.broadcasted_iota(jnp.int32, (128, 256), 1)
     from_u = lax.broadcasted_iota(jnp.int32, (128, 256), 0)
-
-    def halves(a):
-        hi = a.astype(bf16)
-        return hi, (a - hi.astype(f32)).astype(bf16)
-
     flat = jnp.zeros((16, 256), f32)
     for v in range(CROP):
         spread = jnp.where((spot == from_u * CROP + v) & (from_u < CROP), 1.0, 0.0).astype(bf16)
-        for part in halves(lg[v * 16:(v + 1) * 16]):
+        for part in halves(lg[v * 16 : (v + 1) * 16]):
             flat = flat + jnp.dot(part, spread, preferred_element_type=f32)
     flat = jnp.where(lax.broadcasted_iota(jnp.int32, (16, 256), 1) < CROP * CROP, flat, 1.0)
     used = lax.broadcasted_iota(jnp.int32, (16, 16), 1) < cnt
-    sent = jnp.where((own[0] == lax.broadcasted_iota(jnp.int32, (16, 16), 0)) & used, 1.0, 0.0).astype(bf16)
+    sent = (own[0] == lax.broadcasted_iota(jnp.int32, (16, 16), 0)) & used
+    sent = jnp.where(sent, 1.0, 0.0).astype(bf16)
     routed = jnp.zeros((16, 256), f32)
     for part in halves(flat):
         routed = routed + jnp.dot(sent, part, preferred_element_type=f32)
     for o in range(16):
-        rt[o] = routed[o:o + 1]
-
-    fg[...] = jnp.zeros_like(fg)
-
-    def bwd(src, dst, l):
-        def body(i, c):
-            u0 = i * U
-            acc = None
-            for s in range(3):
-                for t in range(3):
-                    a = jnp.concatenate([src[u0 + q + 2 - s, (2 - t) * 16:(2 - t) * 16 + ROWS, :] for q in range(U)], axis=0)
-                    tap = 3 * s + t
-                    d = lax.dot_general(a, w[l, tap * 256:(tap + 1) * 256, :], (((1,), (1,)), ((), ())), preferred_element_type=f32)
-                    acc = d if acc is None else acc + d
-            for q in range(U):
-                gq = acc[q * ROWS:(q + 1) * ROWS]
-                if l > 0:
-                    dst[u0 + q + 1, 16:240, :] = (gq * D[l - 1, u0 + q].astype(f32)).astype(bf16)
-                else:
-                    u = u0 + q
-                    gq = jnp.where(u < heights, gq, 0.0).astype(bf16)
-                    z = lax.dot_general(pick, gq, (((0,), (0,)), ((), ())), preferred_element_type=f32)
-                    for k in range(16):
-                        fg[gs[0, 0, k, 0] + u] += z[k * 32:(k + 1) * 32]
-            return c
-        lax.fori_loop(0, 14 // U, body, 0)
-    bwd(X, Y, 3)
-    bwd(Y, X, 2)
-    bwd(X, Y, 1)
-    bwd(Y, X, 0)
+        rt[o] = routed[o : o + 1]
     store.wait()
+
 
 def mask_head(geometry, count, owner, soft, feat, conv_w, mask_w):
     V = pl.BlockSpec(memory_space=pltpu.VMEM)
     S = pl.BlockSpec(memory_space=pltpu.SMEM)
-    A = pl.BlockSpec(memory_space=pl.ANY)
+    H = pl.BlockSpec(memory_space=pl.ANY)
     return pl.pallas_call(
-        functools.partial(mask_kernel, 7),
+        mask_kernel,
         out_shape=(
             jax.ShapeDtypeStruct((32, 32, 256), jnp.float32),
             jax.ShapeDtypeStruct((16, 1, 256), jnp.float32),
             jax.ShapeDtypeStruct((32, 32, 256), jnp.bfloat16),
         ),
-        in_specs=[S, S, V, V, V, V, A, V],
-        out_specs=(V, V, A),
+        in_specs=[S, S, V, V, V, V, H, V],
+        out_specs=(V, V, H),
         scratch_shapes=[
             pltpu.VMEM((16, 256, 256), jnp.bfloat16),
-            pltpu.VMEM((16, 256, 256), jnp.bfloat16),
+            pltpu.VMEM((4, 7, 256, 256), jnp.bfloat16),
             pltpu.VMEM((3, 14, ROWS, 256), jnp.bfloat16),
             pltpu.VMEM((ROWS, 128), jnp.float32),
             pltpu.VMEM((ROWS, 128), jnp.float32),
             pltpu.VMEM((4, 2304, 256), jnp.bfloat16),
+            pltpu.VMEM((4, 2, 768, 256), jnp.bfloat16),
+            pltpu.VMEM((6, 7 * ROWS, 256), jnp.float32),
             pltpu.SemaphoreType.DMA((5,)),
         ],
         compiler_params=pltpu.CompilerParams(vmem_limit_bytes=63 << 20),
@@ -489,13 +542,13 @@
     box_owner,
     soft_target,
 ):
-    cols = jnp.stack([tokens[:, :4].reshape(128, -1), tokens[:, 28:].reshape(128, -1)])
     features = swin(
-        tokens, cols, first_gain, second_gain, joint_weight, merge_weight,
+        tokens, first_gain, second_gain, joint_weight, merge_weight,
         expand_weight, shrink_weight, relative_bias, lateral_weight,
     )
     feature_grad, outgoing, features = mask_head(
-        box_geometry, box_counts, box_owner, soft_target, features, conv_weight, mask_weight
+        box_geometry.transpose(0, 1, 3, 2), box_counts, box_owner, soft_target, features,
+        conv_weight, mask_weight,
     )
     return (features, feature_grad, deal_logits(outgoing))
 

time: 91.4 us -> 76.2 us (0.83)
  Pallas kernels: 85.2 us -> 73.3 us
  local copies, waits for them, and re-layouts: 3.81 us -> 1.3 us
    pallas_call x1, Pallas kernels: 50.2 us -> 37.6 us  [mask_head(): pl.pallas_call(mask_kernel, out_shape=(jax.ShapeDtypeStruct((32, 32, 256)...]
    unnamed x2 -> x1, local copies, waits for them, and re-layouts: 2.65 us -> 1.3 us
    slice x1 -> x0, local copies, waits for them, and re-layouts: 1.1 us -> none  [shards(): tokens[:, :4].reshape(128, -1)]
where the time goes in v1:
time: 76.2 us; the launch traced here: 75.9 us
  Pallas kernels  73.3 us (96%)
  between operations  1.31 us (2%)
  local copies, waits for them, and re-layouts  1.3 us (2%)
    pallas_call x1, Pallas kernels, mask_head(): pl.pallas_call(mask_kernel, out_shape=(jax.ShapeDtypeStruct((32, 32, 256)...  37.6 us
    pallas_call x1, Pallas kernels, swin(): pl.pallas_call(swin_kernel, out_shape=jax.ShapeDtypeStruct((32, 32, 256),...  21.8 us
    pallas_call x1, Pallas kernels, deal_logits(): pl.pallas_call(deal_kernel, out_shape=jax.ShapeDtypeStruct((1, 1, BOX_OWN...  13.9 us

profile of v1, /device:TPU:24, one launch (start us, length us, event | category | flops | bytes accessed | tf_op | source)
XLA Modules:
  0.0 75.9 jit_solution(10129514217542213842)
XLA Ops:
  1.3 21.8 %shard_map.166.feat = bf16[32,32,256]{2,1,0:T(8,128)(2,1)} custom-call(bf16[32,32,384]{2,1,0:T(8,128)(2,1)} %tok.1, f32[384]{0:T(512)} %g1.1, f32[384]{0:T(512)} %g2.1, bf16[384,1152]{1,0:T(8,128)(2,1)} %wj_h.1, bf16[384,384]{1,0:T(8,128)(2,1)} %wm_h.1, bf16[384,1536]{1,0:T(8,128)(2,1)} %we_h.1, bf16[1536,384]{1,0:T(8,128)(2,1)} %ws_h.1, ...), custom_call_target="tpu_custom_call" | custom-call | tf_op jit(solution)/shard_map/pallas_call | solution.py:226
  23.1 37.6 %shard_map.167 = (f32[32,32,256]{2,1,0:T(8,128)}, f32[16,1,256]{2,1,0:T(1,128)}, bf16[32,32,256]{2,1,0:T(8,128)(2,1)}) custom-call(s32[1,1,4,16]{3,2,1,0:T(4,128)} %bitcast.1, s32[1,1]{1,0:T(1,128)S(6)} %copy.19.cs, s32[1,1,4,16]{3,2,1,0:T(4,128)} %bitcast.2, s32[1,1,16]{2,1,0:T(1,128)} %own.1, bf16[1,1,16,196]{3,2,1,0:T(8,128)(2,1)} %soft.1, ...), custom_call_target="tpu_custom_call" | custom-call | tf_op jit(solution)/shard_map/pallas_call | solution.py:448
  60.7 13.9 %shard_map.168 = f32[1,1,8,196]{3,2,1,0:T(8,128)} custom-call(f32[16,1,256]{2,1,0:T(1,128)} %get-tuple-element.8.outgoing), custom_call_target="tpu_custom_call" | custom-call | tf_op jit(solution)/shard_map/pallas_call | solution.py:514
  74.6 1.3 %copy.20 = f32[1,1,8,196]{3,2,1,0:T(8,128)} copy(f32[1,1,8,196]{3,2,1,0:T(8,128)} %shard_map.168) | data formatting | bytes 12544

commit v2 on v1

--- a/solution.py
+++ b/solution.py
@@ -263,27 +263,13 @@
     return hi, (a - hi.astype(jnp.float32)).astype(jnp.bfloat16)
 
 
-def mask_kernel(gs, cs, geom, own, soft, feat, w_h, mw, fg, rt, feat_out, A, T, D, tgt, lg, w, V, P, sem):
-    f32, bf16 = jnp.float32, jnp.bfloat16
-    cnt = cs[0, 0]
-    loads = [pltpu.make_async_copy(w_h.at[n], w.at[n], sem.at[n]) for n in range(4)]
-    for load in loads:
-        load.start()
-    store = pltpu.make_async_copy(feat, feat_out, sem.at[4])
-    store.start()
-    zrow = jnp.zeros((256, 256), bf16)
-    A[0] = zrow
-    A[15] = zrow
-    for u in range(1, 15):
-        A[u, 0:16, :] = zrow[0:16]
-        A[u, 240:256, :] = zrow[0:16]
-    g = geom[0, 0]
+def placement(g, cnt):
     valid = lax.broadcasted_iota(jnp.int32, (16, 1), 0) < cnt
+    same = lax.broadcasted_iota(jnp.int32, (16, 16), 0) == lax.broadcasted_iota(
+        jnp.int32, (16, 16), 1
+    )
 
     def column(n):
-        same = lax.broadcasted_iota(jnp.int32, (16, 16), 0) == lax.broadcasted_iota(
-            jnp.int32, (16, 16), 1
-        )
         return jnp.sum(jnp.where(same, g[n : n + 1], 0), axis=1, keepdims=True)
 
     def rep(col):
@@ -296,8 +282,39 @@
     in_w = vv < widths
     target = jnp.where(in_w, kk * 32 + lefts + vv, -1)
     lane = lax.broadcasted_iota(jnp.int32, (ROWS, 512), 1)
-    pick = jnp.where(lane == target, 1.0, 0.0).astype(bf16)
-
+    pick = jnp.where(lane == target, 1.0, 0.0).astype(jnp.bfloat16)
+    return pick, in_w, heights
+
+
+def mask_kernel(gs, cs, geom, own, soft, feat, w_h, mw, G, out, A, T, D, tgt, lg, w, V, P, rt, recv, sem, send_sem, recv_sem):
+    f32, bf16 = jnp.float32, jnp.bfloat16
+    cnt = cs[0, 0]
+    loads = [pltpu.make_async_copy(w_h.at[n], w.at[n], sem.at[n]) for n in range(4)]
+    for load in loads:
+        load.start()
+    me, n_row = lax.axis_index("row"), lax.axis_size("row")
+    col_at = lax.axis_index("col")
+    barrier = pltpu.get_barrier_semaphore()
+    for d in range(1, 16):
+        pl.semaphore_signal(
+            barrier, inc=1, device_id=(lax.rem(me + d, n_row), col_at), device_id_type=MESH
+        )
+
+    def copy_to(d, slot):
+        peer = lax.rem(me + d, n_row)
+        return pltpu.make_async_remote_copy(
+            src_ref=rt.at[peer], dst_ref=recv.at[slot],
+            send_sem=send_sem.at[d], recv_sem=recv_sem.at[d],
+            device_id=(peer, col_at), device_id_type=MESH,
+        )
+
+    zrow = jnp.zeros((256, 256), bf16)
+    A[0] = zrow
+    A[15] = zrow
+    for u in range(1, 15):
+        A[u, 0:16, :] = zrow[0:16]
+        A[u, 240:256, :] = zrow[0:16]
+    pick, in_w, heights = placement(geom[0, 0], cnt)
     soft_rows = soft[0, 0]
     cell = lax.broadcasted_iota(jnp.int32, (CROP * CROP, 128), 0)
     step = lax.broadcasted_iota(jnp.int32, (CROP * CROP, 128), 1)
@@ -394,7 +411,6 @@
         if l < 3:
             loads[l + 1].wait()
             taps(l + 1)
-    fg[...] = jnp.zeros_like(fg)
     state[1]()
 
     def products(l):
@@ -406,21 +422,6 @@
     def rows_of(m, odd):
         sl = slice(m * ROWS, (m + 1) * ROWS)
         return P[1, sl] - P[2, sl] - P[3, sl] if odd else P[0, sl] + P[1, sl] + P[2, sl]
-
-    def back(i, c):
-        l = 3 - i
-        products(l)
-        for u in range(CROP):
-            A[u + 1, 16:240, :] = (rows_of(u // 2, u % 2) * D[l - 1, u].astype(f32)).astype(bf16)
-        return c
-
-    lax.fori_loop(0, 3, back, 0)
-    products(0)
-    for u in range(CROP):
-        grad = jnp.where(u < heights, rows_of(u // 2, u % 2), 0.0).astype(bf16)
-        z = lax.dot_general(pick, grad, (((0,), (0,)), ((), ())), preferred_element_type=f32)
-        for k in range(16):
-            fg[gs[0, 0, 0, k] + u] += z[k * 32 : (k + 1) * 32]
 
     spot = lax.broadcasted_iota(jnp.int32, (128, 256), 1)
     from_u = lax.broadcasted_iota(jnp.int32, (128, 256), 0)
@@ -438,22 +439,75 @@
         routed = routed + jnp.dot(sent, part, preferred_element_type=f32)
     for o in range(16):
         rt[o] = routed[o : o + 1]
-    store.wait()
+    recv[me] = rt[me]
+    pl.semaphore_wait(barrier, 15)
+
+    def back(i, c):
+        l = 3 - i
+
+        @pl.when(i == 1)
+        def _():
+            for d in range(1, 16):
+                copy_to(d, me).start()
+
+        products(l)
+        for u in range(CROP):
+            A[u + 1, 16:240, :] = (rows_of(u // 2, u % 2) * D[l - 1, u].astype(f32)).astype(bf16)
+        return c
+
+    lax.fori_loop(0, 3, back, 0)
+    products(0)
+    for u in range(CROP):
+        G[u] = jnp.where(u < heights, rows_of(u // 2, u % 2), 0.0).astype(bf16)
+
+    for d in range(1, 16):
+        copy_to(d, lax.rem(me + n_row - d, n_row)).wait()
+    got = jnp.concatenate([recv[i] for i in range(16)], axis=0)
+    flag = jnp.where(got[:, 255:256] > 0.5, 1.0, 0.0)
+    later = lax.broadcasted_iota(jnp.int32, (16, 16), 0) > lax.broadcasted_iota(
+        jnp.int32, (16, 16), 1
+    )
+    place = jnp.dot(
+        jnp.where(later, 1.0, 0.0).astype(bf16),
+        jnp.broadcast_to(flag, (16, 128)).astype(bf16),
+        preferred_element_type=f32,
+    )[:, 0:1]
+    rows = [
+        jnp.sum(jnp.where((place == float(i)) & (flag > 0.5), got, 0.0), axis=0, keepdims=True)
+        for i in range(BOX_OWN)
+    ]
+    out[0, 0] = jnp.concatenate(rows, axis=0)[:, 0 : CROP * CROP]
+
+
+def place_kernel(gs, cs, geom, G, logits, feat, fg, logits_out, feat_out, sem):
+    load = pltpu.make_async_copy(feat, feat_out, sem.at[0])
+    load.start()
+    pick, _, _ = placement(geom[0, 0], cs[0, 0])
+    logits_out[...] = logits[...]
+    fg[...] = jnp.zeros_like(fg)
+
+    def put(u, c):
+        z = lax.dot_general(pick, G[u], (((0,), (0,)), ((), ())), preferred_element_type=jnp.float32)
+        for k in range(16):
+            fg[gs[0, 0, 0, k] + u] += z[k * 32 : (k + 1) * 32]
+        return c
+
+    lax.fori_loop(0, CROP, put, 0)
+    load.wait()
 
 
 def mask_head(geometry, count, owner, soft, feat, conv_w, mask_w):
     V = pl.BlockSpec(memory_space=pltpu.VMEM)
     S = pl.BlockSpec(memory_space=pltpu.SMEM)
     H = pl.BlockSpec(memory_space=pl.ANY)
-    return pl.pallas_call(
+    grads, logits = pl.pallas_call(
         mask_kernel,
         out_shape=(
-            jax.ShapeDtypeStruct((32, 32, 256), jnp.float32),
-            jax.ShapeDtypeStruct((16, 1, 256), jnp.float32),
-            jax.ShapeDtypeStruct((32, 32, 256), jnp.bfloat16),
+            jax.ShapeDtypeStruct((CROP, ROWS, 256), jnp.bfloat16),
+            jax.ShapeDtypeStruct((1, 1, BOX_OWN, CROP * CROP), jnp.float32),
         ),
         in_specs=[S, S, V, V, V, V, H, V],
-        out_specs=(V, V, H),
+        out_specs=(V, V),
         scratch_shapes=[
             pltpu.VMEM((16, 256, 256), jnp.bfloat16),
             pltpu.VMEM((4, 7, 256, 256), jnp.bfloat16),
@@ -463,66 +517,28 @@
             pltpu.VMEM((4, 2304, 256), jnp.bfloat16),
             pltpu.VMEM((4, 2, 768, 256), jnp.bfloat16),
             pltpu.VMEM((6, 7 * ROWS, 256), jnp.float32),
-            pltpu.SemaphoreType.DMA((5,)),
-        ],
-        compiler_params=pltpu.CompilerParams(vmem_limit_bytes=63 << 20),
-    )(geometry, count, geometry, owner, soft, feat, conv_w, mask_w)
-
-
-def deal_kernel(outgoing, out, recv, send_sem, recv_sem):
-    me, n = lax.axis_index("row"), lax.axis_size("row")
-    col = lax.axis_index("col")
-    barrier = pltpu.get_barrier_semaphore()
-    for d in range(1, 16):
-        pl.semaphore_signal(
-            barrier, inc=1, device_id=(lax.rem(me + d, n), col), device_id_type=MESH
-        )
-    pl.semaphore_wait(barrier, 15)
-
-    def copy_to(d, slot):
-        peer = lax.rem(me + d, n)
-        return pltpu.make_async_remote_copy(
-            src_ref=outgoing.at[peer], dst_ref=recv.at[slot],
-            send_sem=send_sem.at[d], recv_sem=recv_sem.at[d],
-            device_id=(peer, col), device_id_type=MESH,
-        )
-
-    for d in range(1, 16):
-        copy_to(d, me).start()
-    recv[me] = outgoing[me]
-    for d in range(1, 16):
-        copy_to(d, lax.rem(me + n - d, n)).wait()
-    got = jnp.concatenate([recv[i] for i in range(16)], axis=0)
-    flag = jnp.where(got[:, 255:256] > 0.5, 1.0, 0.0)
-    later = lax.broadcasted_iota(jnp.int32, (16, 16), 0) > lax.broadcasted_iota(
-        jnp.int32, (16, 16), 1
-    )
-    place = jnp.dot(
-        jnp.where(later, 1.0, 0.0).astype(jnp.bfloat16),
-        jnp.broadcast_to(flag, (16, 128)).astype(jnp.bfloat16),
-        preferred_element_type=jnp.float32,
-    )[:, 0:1]
-    rows = [
-        jnp.sum(jnp.where((place == float(i)) & (flag > 0.5), got, 0.0), axis=0, keepdims=True)
-        for i in range(BOX_OWN)
-    ]
-    out[0, 0] = jnp.concatenate(rows, axis=0)[:, 0 : CROP * CROP]
-
-
-def deal_logits(outgoing):
-    V = pl.BlockSpec(memory_space=pltpu.VMEM)
-    return pl.pallas_call(
-        deal_kernel,
-        out_shape=jax.ShapeDtypeStruct((1, 1, BOX_OWN, CROP * CROP), jnp.float32),
-        in_specs=[V],
-        out_specs=V,
-        scratch_shapes=[
             pltpu.VMEM((16, 1, 256), jnp.float32),
+            pltpu.VMEM((16, 1, 256), jnp.float32),
+            pltpu.SemaphoreType.DMA((4,)),
             pltpu.SemaphoreType.DMA((16,)),
             pltpu.SemaphoreType.DMA((16,)),
         ],
-        compiler_params=pltpu.CompilerParams(collective_id=1, has_side_effects=True),
-    )(outgoing)
+        compiler_params=pltpu.CompilerParams(
+            vmem_limit_bytes=63 << 20, collective_id=1, has_side_effects=True
+        ),
+    )(geometry, count, geometry, owner, soft, feat, conv_w, mask_w)
+    return pl.pallas_call(
+        place_kernel,
+        out_shape=(
+            jax.ShapeDtypeStruct((32, 32, 256), jnp.float32),
+            jax.ShapeDtypeStruct((1, 1, BOX_OWN, CROP * CROP), jnp.float32),
+            jax.ShapeDtypeStruct((32, 32, 256), jnp.bfloat16),
+        ),
+        in_specs=[S, S, V, V, V, V],
+        out_specs=(V, V, H),
+        scratch_shapes=[pltpu.SemaphoreType.DMA((1,))],
+        compiler_params=pltpu.CompilerParams(vmem_limit_bytes=63 << 20),
+    )(geometry, count, geometry, grads, logits, feat)
 
 
 def shards(
@@ -546,11 +562,11 @@
         tokens, first_gain, second_gain, joint_weight, merge_weight,
         expand_weight, shrink_weight, relative_bias, lateral_weight,
     )
-    feature_grad, outgoing, features = mask_head(
+    feature_grad, logits, features = mask_head(
         box_geometry.transpose(0, 1, 3, 2), box_counts, box_owner, soft_target, features,
         conv_weight, mask_weight,
     )
-    return (features, feature_grad, deal_logits(outgoing))
+    return (features, feature_grad, logits)
 
 
 def solution(mesh):

time: 76.2 us -> 69.8 us (0.916)
  the two profiles are of different devices: /device:TPU:24 before, /device:TPU:7 now
where the time goes in v2:
time: 69.8 us; the launch traced here: 69.6 us
  Pallas kernels  68.1 us (98%)
  between operations  1.48 us (2%)
    pallas_call x1, Pallas kernels, mask_head(): pl.pallas_call(mask_kernel, out_shape=(jax.ShapeDtypeStruct((CROP, ROWS,...  36.6 us
    pallas_call x1, Pallas kernels, swin(): pl.pallas_call(swin_kernel, out_shape=jax.ShapeDtypeStruct((32, 32, 256),...  24.7 us
    pallas_call x1, Pallas kernels, mask_head(): pl.pallas_call(place_kernel, out_shape=(jax.ShapeDtypeStruct((32, 32, 256...  6.89 us

profile of v2, /device:TPU:7, one launch (start us, length us, event | category | flops | bytes accessed | tf_op | source)
XLA Modules:
  0.0 69.6 jit_solution(7150533609262566012)
XLA Ops:
  1.3 24.7 %shard_map.166.feat = bf16[32,32,256]{2,1,0:T(8,128)(2,1)} custom-call(bf16[32,32,384]{2,1,0:T(8,128)(2,1)} %tok.1, f32[384]{0:T(512)} %g1.1, f32[384]{0:T(512)} %g2.1, bf16[384,1152]{1,0:T(8,128)(2,1)} %wj_h.1, bf16[384,384]{1,0:T(8,128)(2,1)} %wm_h.1, bf16[384,1536]{1,0:T(8,128)(2,1)} %we_h.1, bf16[1536,384]{1,0:T(8,128)(2,1)} %ws_h.1, ...), custom_call_target="tpu_custom_call" | custom-call | tf_op jit(solution)/shard_map/pallas_call | solution.py:226
  26.0 36.6 %shard_map.167 = (bf16[14,224,256]{2,1,0:T(8,128)(2,1)}, f32[1,1,8,196]{3,2,1,0:T(8,128)}) custom-call(s32[1,1,4,16]{3,2,1,0:T(4,128)} %bitcast.1, s32[1,1]{1,0:T(1,128)S(6)} %copy.18.cs, s32[1,1,4,16]{3,2,1,0:T(4,128)} %bitcast.2, s32[1,1,16]{2,1,0:T(1,128)} %own.1, bf16[1,1,16,196]{3,2,1,0:T(8,128)(2,1)} %soft.1, bf16[32,32,256]{2,1,0:T(8,128)(2,1)} %shard_map.166.feat, ...), custom_call_target="tpu_custom_call" | custom-call | tf_op jit(solution)/shard_map/pallas_call | solution.py:503
  62.6 6.9 %shard_map.168 = (f32[32,32,256]{2,1,0:T(8,128)}, f32[1,1,8,196]{3,2,1,0:T(8,128)}, bf16[32,32,256]{2,1,0:T(8,128)(2,1)}) custom-call(s32[1,1,4,16]{3,2,1,0:T(4,128)} %bitcast.3, s32[1,1]{1,0:T(1,128)S(6)} %copy.18.cs, s32[1,1,4,16]{3,2,1,0:T(4,128)} %bitcast.4, bf16[14,224,256]{2,1,0:T(8,128)(2,1)} %get-tuple-element.8.G, ...), custom_call_target="tpu_custom_call" | custom-call | tf_op jit(solution)/shard_map/pallas_call | solution.py:530

commit v3 on v2

--- a/solution.py
+++ b/solution.py
@@ -200,7 +200,7 @@
     lax.fori_loop(0, 2, ends, 0)
     for load in loads[2:]:
         load.wait()
-    R = 16
+    R = 32
 
     def tail(c, carry):
         r0 = c * R
@@ -479,20 +479,23 @@
     out[0, 0] = jnp.concatenate(rows, axis=0)[:, 0 : CROP * CROP]
 
 
-def place_kernel(gs, cs, geom, G, logits, feat, fg, logits_out, feat_out, sem):
+def place_kernel(gs, cs, geom, G, logits, feat, fg, logits_out, feat_out, PT, sem):
     load = pltpu.make_async_copy(feat, feat_out, sem.at[0])
     load.start()
     pick, _, _ = placement(geom[0, 0], cs[0, 0])
+    PT[...] = pick.astype(jnp.float32).T.astype(jnp.bfloat16)
     logits_out[...] = logits[...]
     fg[...] = jnp.zeros_like(fg)
 
-    def put(u, c):
-        z = lax.dot_general(pick, G[u], (((0,), (0,)), ((), ())), preferred_element_type=jnp.float32)
-        for k in range(16):
-            fg[gs[0, 0, 0, k] + u] += z[k * 32 : (k + 1) * 32]
+    def put(i, c):
+        for q in range(2):
+            u = 2 * i + q
+            z = jnp.dot(PT[...], G[u], preferred_element_type=jnp.float32)
+            for k in range(16):
+                fg[gs[0, 0, 0, k] + u] += z[k * 32 : (k + 1) * 32]
         return c
 
-    lax.fori_loop(0, CROP, put, 0)
+    lax.fori_loop(0, CROP // 2, put, 0)
     load.wait()
 
 
@@ -536,7 +539,7 @@
         ),
         in_specs=[S, S, V, V, V, V],
         out_specs=(V, V, H),
-        scratch_shapes=[pltpu.SemaphoreType.DMA((1,))],
+        scratch_shapes=[pltpu.VMEM((512, ROWS), jnp.bfloat16), pltpu.SemaphoreType.DMA((1,))],
         compiler_params=pltpu.CompilerParams(vmem_limit_bytes=63 << 20),
     )(geometry, count, geometry, grads, logits, feat)
 

time: 69.8 us -> 67.9 us (0.973)
  Pallas kernels: 68.1 us -> 66.3 us
    pallas_call x1, Pallas kernels: 6.89 us -> 5.49 us  [mask_head(): pl.pallas_call(place_kernel, out_shape=(jax.ShapeDtypeStruct((32, 32, 256...]
where the time goes in v3:
time: 67.9 us; the launch traced here: 67.8 us
  Pallas kernels  66.3 us (98%)
  between operations  1.48 us (2%)
    pallas_call x1, Pallas kernels, mask_head(): pl.pallas_call(mask_kernel, out_shape=(jax.ShapeDtypeStruct((CROP, ROWS,...  36.6 us
    pallas_call x1, Pallas kernels, swin(): pl.pallas_call(swin_kernel, out_shape=jax.ShapeDtypeStruct((32, 32, 256),...  24.3 us
    pallas_call x1, Pallas kernels, mask_head(): pl.pallas_call(place_kernel, out_shape=(jax.ShapeDtypeStruct((32, 32, 256...  5.49 us

profile of v3, /device:TPU:7, one launch (start us, length us, event | category | flops | bytes accessed | tf_op | source)
XLA Modules:
  0.0 67.8 jit_solution(3005544862108582266)
XLA Ops:
  1.3 24.3 %shard_map.166.feat = bf16[32,32,256]{2,1,0:T(8,128)(2,1)} custom-call(bf16[32,32,384]{2,1,0:T(8,128)(2,1)} %tok.1, f32[384]{0:T(512)} %g1.1, f32[384]{0:T(512)} %g2.1, bf16[384,1152]{1,0:T(8,128)(2,1)} %wj_h.1, bf16[384,384]{1,0:T(8,128)(2,1)} %wm_h.1, bf16[384,1536]{1,0:T(8,128)(2,1)} %we_h.1, bf16[1536,384]{1,0:T(8,128)(2,1)} %ws_h.1, ...), custom_call_target="tpu_custom_call" | custom-call | tf_op jit(solution)/shard_map/pallas_call | solution.py:226
  25.5 36.6 %shard_map.167 = (bf16[14,224,256]{2,1,0:T(8,128)(2,1)}, f32[1,1,8,196]{3,2,1,0:T(8,128)}) custom-call(s32[1,1,4,16]{3,2,1,0:T(4,128)} %bitcast.1, s32[1,1]{1,0:T(1,128)S(6)} %copy.18.cs, s32[1,1,4,16]{3,2,1,0:T(4,128)} %bitcast.2, s32[1,1,16]{2,1,0:T(1,128)} %own.1, bf16[1,1,16,196]{3,2,1,0:T(8,128)(2,1)} %soft.1, bf16[32,32,256]{2,1,0:T(8,128)(2,1)} %shard_map.166.feat, ...), custom_call_target="tpu_custom_call" | custom-call | tf_op jit(solution)/shard_map/pallas_call | solution.py:506
  62.1 5.5 %shard_map.168 = (f32[32,32,256]{2,1,0:T(8,128)}, f32[1,1,8,196]{3,2,1,0:T(8,128)}, bf16[32,32,256]{2,1,0:T(8,128)(2,1)}) custom-call(s32[1,1,4,16]{3,2,1,0:T(4,128)} %bitcast.3, s32[1,1]{1,0:T(1,128)S(6)} %copy.18.cs, s32[1,1,4,16]{3,2,1,0:T(4,128)} %bitcast.4, bf16[14,224,256]{2,1,0:T(8,128)(2,1)} %get-tuple-element.8.G, ...), custom_call_target="tpu_custom_call" | custom-call | tf_op jit(solution)/shard_map/pallas_call | solution.py:533

commit v4 on v3

--- a/solution.py
+++ b/solution.py
@@ -61,10 +61,6 @@
         def _(peer=peer):
             pl.semaphore_signal(barrier, inc=1, device_id=peer, device_id_type=MESH)
 
-    near_rows = jnp.where(row_at > 0, 1, 0) + jnp.where(row_at < row_n - 1, 1, 0) + 1
-    near_cols = jnp.where(col_at > 0, 1, 0) + jnp.where(col_at < col_n - 1, 1, 0) + 1
-    pl.semaphore_wait(barrier, near_rows * near_cols - 1)
-
     def parts(dr, dc):
         if dc == 0:
             return (tok.at[0:4], bottom) if dr < 0 else (tok.at[28:32], top)
@@ -81,24 +77,29 @@
             device_id=peer, device_id_type=MESH,
         )
 
+    def fill(i, carry):
+        for q in range(8):
+            r = i * 8 + q
+            E[r + 4, 4:36, :] = tok[r].astype(f32)
+        return carry
+
+    lax.fori_loop(0, 4, fill, 0)
+    near_rows = jnp.where(row_at > 0, 1, 0) + jnp.where(row_at < row_n - 1, 1, 0) + 1
+    near_cols = jnp.where(col_at > 0, 1, 0) + jnp.where(col_at < col_n - 1, 1, 0) + 1
+    pl.semaphore_wait(barrier, near_rows * near_cols - 1)
+
     for n, (dr, dc, there, peer) in enumerate(around):
 
         @pl.when(there)
         def _(n=n, dr=dr, dc=dc, peer=peer):
             copy_to(n, dr, dc, peer).start()
 
-    def fill(r, carry):
-        E[r + 4, 4:36, :] = tok[r].astype(f32)
-        return carry
-
-    lax.fori_loop(0, 32, fill, 0)
     loads[0].wait()
     loads[1].wait()
     for c in range(6):
         BB[c] = jnp.concatenate([rb[2 * c], rb[2 * c + 1]], axis=1)
     lane = lax.broadcasted_iota(jnp.int32, (64, 128), 1)
     head_of = lane // 32
-    zero = jnp.zeros((64, 128), bf16)
     for h in range(4):
         ON[h * 64 : (h + 1) * 64] = jnp.where(head_of == h, 1.0, 0.0).astype(bf16)
     low = lane < 64
@@ -135,7 +136,7 @@
                 q = J[sl, g * 128 : (g + 1) * 128]
                 k = J[sl, 384 + g * 128 : 384 + (g + 1) * 128]
                 v = J[sl, 768 + g * 128 : 768 + (g + 1) * 128]
-                kb = jnp.concatenate([jnp.where(head_of == h, k, zero) for h in range(4)], axis=0)
+                kb = jnp.concatenate([k] * 4, axis=0) * ON[...]
                 s = lax.dot_general(q, kb, (((1,), (1,)), ((), ())), preferred_element_type=f32)
                 es = []
                 for c in range(2):
@@ -145,7 +146,7 @@
                     m1 = jnp.max(jnp.where(low, -3e38, b), axis=1, keepdims=True)
                     es.append(jnp.exp(b - jnp.where(low, m0, m1)).astype(bf16))
                 p = jnp.concatenate(es, axis=1)
-                vb = jnp.concatenate([jnp.where(head_of == h, v, zero) for h in range(4)], axis=0)
+                vb = jnp.concatenate([v] * 4, axis=0) * ON[...]
                 o = jnp.dot(p, jnp.concatenate([vb, ON[...]], axis=1), preferred_element_type=f32)
                 o = o[:, 0:128] / o[:, 128:256]
                 ME[pl.ds(wi * 8, 8), j * 8 : (j + 1) * 8, g * 128 : (g + 1) * 128] = o.reshape(8, 8, 128)
@@ -322,14 +323,16 @@
         spread = jnp.where(cell == step * CROP + v, 1.0, 0.0).astype(bf16)
         tgt[v * 16 : (v + 1) * 16] = jnp.dot(soft_rows, spread, preferred_element_type=f32)
 
-    def gather(u, c):
-        strips = jnp.concatenate([feat[gs[0, 0, 0, k] + u] for k in range(16)], axis=0)
-        crop = jnp.dot(pick, strips, preferred_element_type=f32)
-        crop = jnp.where(u < heights, crop, 0.0)
-        A[u + 1, 16:240, :] = crop.astype(bf16)
+    def gather(i, c):
+        for q in range(2):
+            u = 2 * i + q
+            strips = jnp.concatenate([feat[gs[0, 0, 0, k] + u] for k in range(16)], axis=0)
+            crop = jnp.dot(pick, strips, preferred_element_type=f32)
+            crop = jnp.where(u < heights, crop, 0.0)
+            A[u + 1, 16:240, :] = crop.astype(bf16)
         return c
 
-    lax.fori_loop(0, CROP, gather, 0)
+    lax.fori_loop(0, CROP // 2, gather, 0)
     lg[...] = jnp.zeros_like(lg)
 
     def form(j):

time: 67.9 us -> 66.5 us (0.979)
  Pallas kernels: 66.3 us -> 64.8 us
    pallas_call x1, Pallas kernels: 36.6 us -> 35.4 us  [mask_head(): pl.pallas_call(mask_kernel, out_shape=(jax.ShapeDtypeStruct((CROP, ROWS,...]
where the time goes in v4:
time: 66.5 us; the launch traced here: 66.3 us
  Pallas kernels  64.8 us (97%)
  between operations  1.48 us (2%)
    pallas_call x1, Pallas kernels, mask_head(): pl.pallas_call(mask_kernel, out_shape=(jax.ShapeDtypeStruct((CROP, ROWS,...  35.4 us
    pallas_call x1, Pallas kernels, swin(): pl.pallas_call(swin_kernel, out_shape=jax.ShapeDtypeStruct((32, 32, 256),...  24 us
    pallas_call x1, Pallas kernels, mask_head(): pl.pallas_call(place_kernel, out_shape=(jax.ShapeDtypeStruct((32, 32, 256...  5.44 us

profile of v4, /device:TPU:7, one launch (start us, length us, event | category | flops | bytes accessed | tf_op | source)
XLA Modules:
  0.0 66.3 jit_solution(296954600583916536)
XLA Ops:
  1.3 24.0 %shard_map.166.feat = bf16[32,32,256]{2,1,0:T(8,128)(2,1)} custom-call(bf16[32,32,384]{2,1,0:T(8,128)(2,1)} %tok.1, f32[384]{0:T(512)} %g1.1, f32[384]{0:T(512)} %g2.1, bf16[384,1152]{1,0:T(8,128)(2,1)} %wj_h.1, bf16[384,384]{1,0:T(8,128)(2,1)} %wm_h.1, bf16[384,1536]{1,0:T(8,128)(2,1)} %we_h.1, bf16[1536,384]{1,0:T(8,128)(2,1)} %ws_h.1, ...), custom_call_target="tpu_custom_call" | custom-call | tf_op jit(solution)/shard_map/pallas_call | solution.py:227
  25.2 35.4 %shard_map.167 = (bf16[14,224,256]{2,1,0:T(8,128)(2,1)}, f32[1,1,8,196]{3,2,1,0:T(8,128)}) custom-call(s32[1,1,4,16]{3,2,1,0:T(4,128)} %bitcast.1, s32[1,1]{1,0:T(1,128)S(6)} %copy.18.cs, s32[1,1,4,16]{3,2,1,0:T(4,128)} %bitcast.2, s32[1,1,16]{2,1,0:T(1,128)} %own.1, bf16[1,1,16,196]{3,2,1,0:T(8,128)(2,1)} %soft.1, bf16[32,32,256]{2,1,0:T(8,128)(2,1)} %shard_map.166.feat, ...), custom_call_target="tpu_custom_call" | custom-call | tf_op jit(solution)/shard_map/pallas_call | solution.py:509
  60.7 5.4 %shard_map.168 = (f32[32,32,256]{2,1,0:T(8,128)}, f32[1,1,8,196]{3,2,1,0:T(8,128)}, bf16[32,32,256]{2,1,0:T(8,128)(2,1)}) custom-call(s32[1,1,4,16]{3,2,1,0:T(4,128)} %bitcast.3, s32[1,1]{1,0:T(1,128)S(6)} %copy.18.cs, s32[1,1,4,16]{3,2,1,0:T(4,128)} %bitcast.4, bf16[14,224,256]{2,1,0:T(8,128)(2,1)} %get-tuple-element.8.G, ...), custom_call_target="tpu_custom_call" | custom-call | tf_op jit(solution)/shard_map/pallas_call | solution.py:536

commit v5 on v4

--- a/solution.py
+++ b/solution.py
@@ -192,7 +192,7 @@
         windows(n + 1, (0, 4))
         return carry
 
-    lax.fori_loop(0, 3, sides, 0)
+    lax.fori_loop(0, 3, sides, 0, unroll=True)
 
     def ends(n, carry):
         windows(n * 4, (0, 1, 2, 3, 4))
@@ -324,15 +324,15 @@
         tgt[v * 16 : (v + 1) * 16] = jnp.dot(soft_rows, spread, preferred_element_type=f32)
 
     def gather(i, c):
-        for q in range(2):
-            u = 2 * i + q
+        for q in range(7):
+            u = 7 * i + q
             strips = jnp.concatenate([feat[gs[0, 0, 0, k] + u] for k in range(16)], axis=0)
             crop = jnp.dot(pick, strips, preferred_element_type=f32)
             crop = jnp.where(u < heights, crop, 0.0)
             A[u + 1, 16:240, :] = crop.astype(bf16)
         return c
 
-    lax.fori_loop(0, CROP // 2, gather, 0)
+    lax.fori_loop(0, CROP // 7, gather, 0)
     lg[...] = jnp.zeros_like(lg)
 
     def form(j):
@@ -491,14 +491,14 @@
     fg[...] = jnp.zeros_like(fg)
 
     def put(i, c):
-        for q in range(2):
-            u = 2 * i + q
+        for q in range(7):
+            u = 7 * i + q
             z = jnp.dot(PT[...], G[u], preferred_element_type=jnp.float32)
             for k in range(16):
                 fg[gs[0, 0, 0, k] + u] += z[k * 32 : (k + 1) * 32]
         return c
 
-    lax.fori_loop(0, CROP // 2, put, 0)
+    lax.fori_loop(0, CROP // 7, put, 0)
     load.wait()
 
 

time: 66.5 us -> 64.4 us (0.968)
  Pallas kernels: 64.8 us -> 62.7 us
    pallas_call x1, Pallas kernels: 35.4 us -> 34.6 us  [mask_head(): pl.pallas_call(mask_kernel, out_shape=(jax.ShapeDtypeStruct((CROP, ROWS,...]
    pallas_call x1, Pallas kernels: 5.44 us -> 4.72 us  [mask_head(): pl.pallas_call(place_kernel, out_shape=(jax.ShapeDtypeStruct((32, 32, 256...]
where the time goes in v5:
time: 64.4 us; the launch traced here: 64.2 us
  Pallas kernels  62.7 us (97%)
  between operations  1.48 us (2%)
    pallas_call x1, Pallas kernels, mask_head(): pl.pallas_call(mask_kernel, out_shape=(jax.ShapeDtypeStruct((CROP, ROWS,...  34.6 us
    pallas_call x1, Pallas kernels, swin(): pl.pallas_call(swin_kernel, out_shape=jax.ShapeDtypeStruct((32, 32, 256),...  23.4 us
    pallas_call x1, Pallas kernels, mask_head(): pl.pallas_call(place_kernel, out_shape=(jax.ShapeDtypeStruct((32, 32, 256...  4.72 us

profile of v5, /device:TPU:7, one launch (start us, length us, event | category | flops | bytes accessed | tf_op | source)
XLA Modules:
  0.0 64.2 jit_solution(12969562087907455863)
XLA Ops:
  1.3 23.4 %shard_map.166.feat = bf16[32,32,256]{2,1,0:T(8,128)(2,1)} custom-call(bf16[32,32,384]{2,1,0:T(8,128)(2,1)} %tok.1, f32[384]{0:T(512)} %g1.1, f32[384]{0:T(512)} %g2.1, bf16[384,1152]{1,0:T(8,128)(2,1)} %wj_h.1, bf16[384,384]{1,0:T(8,128)(2,1)} %wm_h.1, bf16[384,1536]{1,0:T(8,128)(2,1)} %we_h.1, bf16[1536,384]{1,0:T(8,128)(2,1)} %ws_h.1, ...), custom_call_target="tpu_custom_call" | custom-call | tf_op jit(solution)/shard_map/pallas_call | solution.py:227
  24.7 34.6 %shard_map.167 = (bf16[14,224,256]{2,1,0:T(8,128)(2,1)}, f32[1,1,8,196]{3,2,1,0:T(8,128)}) custom-call(s32[1,1,4,16]{3,2,1,0:T(4,128)} %bitcast.1, s32[1,1]{1,0:T(1,128)S(6)} %copy.18.cs, s32[1,1,4,16]{3,2,1,0:T(4,128)} %bitcast.2, s32[1,1,16]{2,1,0:T(1,128)} %own.1, bf16[1,1,16,196]{3,2,1,0:T(8,128)(2,1)} %soft.1, bf16[32,32,256]{2,1,0:T(8,128)(2,1)} %shard_map.166.feat, ...), custom_call_target="tpu_custom_call" | custom-call | tf_op jit(solution)/shard_map/pallas_call | solution.py:509
  59.3 4.7 %shard_map.168 = (f32[32,32,256]{2,1,0:T(8,128)}, f32[1,1,8,196]{3,2,1,0:T(8,128)}, bf16[32,32,256]{2,1,0:T(8,128)(2,1)}) custom-call(s32[1,1,4,16]{3,2,1,0:T(4,128)} %bitcast.3, s32[1,1]{1,0:T(1,128)S(6)} %copy.18.cs, s32[1,1,4,16]{3,2,1,0:T(4,128)} %bitcast.4, bf16[14,224,256]{2,1,0:T(8,128)(2,1)} %get-tuple-element.8.G, ...), custom_call_target="tpu_custom_call" | custom-call | tf_op jit(solution)/shard_map/pallas_call | solution.py:536
